TPU v7x, 512 devices: a whole 4x8x8 slice. The times are simulated.
512 devices in a mesh: item: 8 (over y), rows: 32 (over z, x_hi, core), hid: 2 (over x_lo).
Axes of the slice: x: 4 (x_hi: 2, x_lo: 2; x = x_hi * 2 + x_lo), y: 8, z: 8, core: 2. Of those that a mesh axis runs over, the one named last changes fastest.
Arguments:
- latents: float32 [16, 32, 2048], P('item', 'rows'), may hold values from -6 to 6
- heights: int32 [16], P('item'), may hold values from 8 to 32, as said below
- widths: int32 [16], P('item'), may hold values from 8 to 32, as said below
- slot_item: int32 [16], P('item'), may hold values from 0 to 15, each once
- step_index: int32 [1], replicated, may hold values from 0 to 27
- cond_table: float32 [16, 5, 1536], replicated, may hold values from -9 to 9
- text_kv: bfloat16 [16, 2, 154, 768], P('item', None, None, 'hid'), may hold values from -175 to 175
- patch_weight: bfloat16 [64, 1536], replicated, may hold values from -0.75 to 0.75
- qkv_weight: bfloat16 [3, 1536, 768], P(None, ('item', 'rows'), 'hid'), may hold values from -0.15625 to 0.15625
- out_weight: bfloat16 [768, 1536], P('hid', ('item', 'rows')), may hold values from -0.21875 to 0.21875
- final_weight: bfloat16 [1536, 64], replicated, may hold values from -0.15625 to 0.15625
Outputs:
- next_latents: float32 [16, 32, 2048], P('item', 'rows')
- denoised: float32 [16, 32, 2048], P('item', 'rows')
Inputs may be any that keep to these rules, and one draw needn't show every extreme that they name: `heights`: every grid has at least 8 rows, and some item has exactly 32. `widths`: every grid has at least 8 columns, and some item has exactly 32. `slot_item`: each request is served by exactly one slot.
All inputs are finite; a program needn't handle non-finite values.
Results may differ from a plain program's by a relative error of at most 0.007.
Values may be sent and summed in bfloat16 or wider, within the bound.
A program may use at most 64 MiB of HBM per device.

v0:
```python
import jax
import jax.numpy as jnp
from jax import lax
from jax.sharding import PartitionSpec as P

HD = 64
STEPS = 28


def sigma_level(position):
    fraction = 1.0 - position / STEPS
    return 3.0 * fraction / (1.0 + 2.0 * fraction)


def position_embed(row_pos, col_count, model_width):
    quarter = model_width // 4
    frequency = 1.0 / 10000.0 ** (jnp.arange(quarter, dtype=jnp.float32) / quarter)
    col_pos = jnp.arange(col_count, dtype=jnp.float32)
    row_angle = row_pos[:, None] * frequency[None, :]
    col_angle = col_pos[:, None] * frequency[None, :]
    row_part = jnp.concatenate([jnp.sin(row_angle), jnp.cos(row_angle)], 1)
    col_part = jnp.concatenate([jnp.sin(col_angle), jnp.cos(col_angle)], 1)
    row_full = jnp.broadcast_to(
        row_part[:, None, :], (row_pos.shape[0], col_count, model_width // 2)
    )
    col_full = col_part[None, :, :]
    return jnp.concatenate([row_full, col_full], 2)


def normalize(values):
    mean_rows = jnp.mean(values, -1, keepdims=True)
    centered = values - mean_rows
    return centered * lax.rsqrt(jnp.mean(centered * centered, -1, keepdims=True) + 1e-06)


def body(
    latents,
    heights,
    widths,
    slot_item,
    step_index,
    cond_table,
    text_kv,
    patch_weight,
    qkv_weight,
    out_weight,
    final_weight,
):
    slot_count = latents.shape[0]
    rows_here = latents.shape[1]
    channels = patch_weight.shape[0]
    model_width = patch_weight.shape[1]
    col_count = latents.shape[2] // channels
    local_width = text_kv.shape[3]
    heads_here = local_width // HD
    text_count = text_kv.shape[2]
    per_slot = rows_here * col_count
    tok_rows = slot_count * per_slot
    row_start = lax.axis_index("rows") * rows_here
    row_pos = (row_start + jnp.arange(rows_here, dtype=jnp.int32)).astype(jnp.float32)
    patches = latents.reshape(tok_rows, channels).astype(jnp.bfloat16)
    embedded = jnp.dot(patches, patch_weight, preferred_element_type=jnp.float32).reshape(
        slot_count, per_slot, model_width
    )
    embedded = embedded + position_embed(row_pos, col_count, model_width)
    entries = cond_table.shape[0]
    chosen = (slot_item[:, None] == jnp.arange(entries, dtype=jnp.int32)[None, :]).astype(
        jnp.float32
    )
    conditions = jnp.dot(
        chosen, cond_table.reshape(entries, 5 * model_width), precision=lax.Precision.HIGHEST
    )
    conditions = conditions.reshape(slot_count, 5, model_width)
    normed = (normalize(embedded) * (1.0 + conditions[:, 1:2, :]) + conditions[:, 0:1, :]).astype(
        jnp.bfloat16
    )
    flat_rows = normed.reshape(tok_rows, model_width)
    projected = jnp.einsum(
        "td,kdh->kth",
        flat_rows,
        lax.all_gather(qkv_weight, ("item", "rows"), axis=1, tiled=True),
        preferred_element_type=jnp.float32,
    )
    projected = projected.astype(jnp.bfloat16)
    queries = projected[0].reshape(slot_count, per_slot, heads_here, HD)
    image_kv = projected[1:].reshape(2, slot_count, rows_here, col_count, local_width)
    score_scale = HD ** (-0.5)
    text_keys = text_kv[:, 0].reshape(slot_count, text_count, heads_here, HD)
    text_vals = text_kv[:, 1].reshape(slot_count, text_count, heads_here, HD)
    text_score = (
        jnp.einsum("sqhd,skhd->shqk", queries, text_keys, preferred_element_type=jnp.float32)
        * score_scale
    )
    first_top = jnp.max(text_score, -1)
    text_weights = jnp.exp(text_score - first_top[..., None])
    first_total = jnp.sum(text_weights, -1)
    first_acc = jnp.einsum(
        "shqk,skhd->shqd",
        text_weights.astype(jnp.bfloat16),
        text_vals,
        preferred_element_type=jnp.float32,
    )
    col_live = jnp.arange(col_count, dtype=jnp.int32)[None, :] < widths[:, None]
    gathered = lax.all_gather(image_kv, "rows", axis=2, tiled=True)
    run_top = first_top
    run_total = first_total
    run_acc = first_acc
    key_rows = gathered.shape[2]
    key_piece = gathered[0].reshape(slot_count, key_rows * col_count, heads_here, HD)
    val_piece = gathered[1].reshape(slot_count, key_rows * col_count, heads_here, HD)
    scores = (
        jnp.einsum("sqhd,skhd->shqk", queries, key_piece, preferred_element_type=jnp.float32)
        * score_scale
    )
    key_index = jnp.arange(key_rows, dtype=jnp.int32)
    live_mask = (key_index[None, :, None] < heights[:, None, None]) & col_live[:, None, :]
    live_mask = live_mask.reshape(slot_count, 1, 1, key_rows * col_count)
    scores = jnp.where(live_mask, scores, -1e30)
    new_top = jnp.maximum(run_top, jnp.max(scores, -1))
    factor = jnp.exp(run_top - new_top)
    weights = jnp.exp(scores - new_top[..., None])
    run_total = run_total * factor + jnp.sum(weights, -1)
    run_acc = run_acc * factor[..., None] + jnp.einsum(
        "shqk,skhd->shqd",
        weights.astype(jnp.bfloat16),
        val_piece,
        preferred_element_type=jnp.float32,
    )
    run_top, run_total, run_acc = (new_top, run_total, run_acc)
    attended = (
        (run_acc / run_total[..., None])
        .transpose(0, 2, 1, 3)
        .reshape(tok_rows, local_width)
        .astype(jnp.bfloat16)
    )
    partial_value = jnp.dot(
        attended,
        lax.all_gather(out_weight, ("item", "rows"), axis=1, tiled=True),
        preferred_element_type=jnp.float32,
    )
    summed = lax.psum(partial_value.astype(jnp.bfloat16), "hid").astype(jnp.float32)
    summed = summed.reshape(slot_count, per_slot, model_width)
    residual = embedded + conditions[:, 2:3, :] * summed
    final_in = (normalize(residual) * (1.0 + conditions[:, 4:5, :]) + conditions[:, 3:4, :]).astype(
        jnp.bfloat16
    )
    velocity = jnp.dot(
        final_in.reshape(tok_rows, model_width), final_weight, preferred_element_type=jnp.float32
    )
    position = step_index[0].astype(jnp.float32)
    sigma_now = sigma_level(position)
    sigma_next = sigma_level(position + 1.0)
    row_global = row_start + jnp.arange(rows_here, dtype=jnp.int32)
    live_patch = (row_global[None, :, None] < heights[:, None, None]) & col_live[:, None, :]
    velocity = velocity.reshape(slot_count, rows_here, col_count, channels)
    live_velocity = jnp.where(live_patch[..., None], velocity, 0.0).reshape(
        slot_count, rows_here, col_count * channels
    )
    next_latents = latents + (sigma_next - sigma_now) * live_velocity
    denoised = latents - sigma_now * live_velocity
    return (next_latents, denoised)


def solution(mesh):
    return jax.shard_map(
        body,
        mesh=mesh,
        in_specs=(
            P("item", "rows", None),
            P("item"),
            P("item"),
            P("item"),
            P(),
            P(),
            P("item", None, None, "hid"),
            P(),
            P(None, ("item", "rows"), "hid"),
            P("hid", ("item", "rows")),
            P(),
        ),
        out_specs=(P("item", "rows", None), P("item", "rows", None)),
        check_vma=False,
    )
```

profile of v0, /device:TPU:1, one launch (start us, length us, event | category | flops | bytes accessed | tf_op | source)
XLA Modules:
  0.0 422.9 jit_solution(1402297968687768749)
XLA Ops:
  7.2 0.0 all-gather.5.cloned.1.call-start
  7.2 1.4 copy.35
  8.6 0.0 all-gather.5.cloned.1.call-update
  8.6 0.0 all-gather.9.cloned.1.call-start
  8.7 0.7 all-gather.9.cloned.1.call-update
  9.4 0.0 all-gather.7.cloned.1.call-start
  9.5 0.1 fusion.49
  9.5 0.2 fusion.42
  9.8 0.8 convert_reduce_fusion
  10.6 0.1 convert_element_type.46
  10.7 1.2 fusion.56
  11.9 0.2 multiply_reduce_fusion.1
  12.1 0.3 fusion.25
  12.4 0.1 add_convert_fusion.1
  12.6 136.8 %all-gather.5.cloned.1.call-done = bf16[3,1536,384]{2,0,1:T(4,128)(2,1)} async-done(((bf16[3,6,384]{2,0,1:T(4,128)(2,1)}), bf16[3,1536,384]{2,0,1:T(4,128)(2,1)}) %all-gather.5.cloned.1.call-update) | async-done | bytes 3538960 | tf_op jit(solution)/shard_map/all_gather | solution.py:81
  149.4 3.1 fusion.20
  152.5 0.6 slice.48
  153.1 0.0 all-gather.7.cloned.1.call-update
  153.2 0.0 all-reduce.2.cloned.1.call-start
  153.2 0.1 broadcast_and_fusion.1
  153.3 0.1 broadcast_and_fusion
  153.4 0.1 and.40
  153.5 0.7 fusion.54
  154.2 0.5 copy.37
  154.7 0.5 copy.39
  155.2 109.8 %all-gather.9.cloned.1.call-done = bf16[256,6,384]{2,1,0:T(8,128)(2,1)} async-done(((bf16[1,6,384]{2,1,0:T(8,128)(2,1)}), bf16[256,6,384]{2,1,0:T(8,128)(2,1)}) %all-gather.9.cloned.1.call-update) | async-done | bytes 1179664 | tf_op jit(solution)/shard_map/all_gather | solution.py:138
  265.0 3.3 reshape.279
  268.3 0.1 reshape_squeeze.15
  268.4 0.3 fusion.57
  268.7 0.2 fusion.28
  268.9 85.4 %all-gather.7.cloned.1.call-done = bf16[2,2,32,32,384]{4,3,2,1,0:T(8,128)(2,1)} async-done(((bf16[2,2,1,32,384]{4,3,2,1,0:T(8,128)(2,1)}), bf16[2,2,32,32,384]{4,3,2,1,0:T(8,128)(2,1)}) %all-gather.7.cloned.1.call-update) | async-done | bytes 3145744 | tf_op jit(solution)/shard_map/all_gather | solution.py:104
  354.4 3.5 fusion.53
  357.8 3.7 reshape_squeeze.18
  361.6 3.4 fusion.58
  365.0 5.9 %reshape_squeeze.19 = bf16[2,1024,6,64]{3,2,1,0:T(8,128)(2,1)} reshape(bf16[1,2,32,32,384]{4,3,2,1,0:T(8,128)(2,1)} %get-tuple-element.5) | data formatting | bytes 3145728 | tf_op jit(solution)/shard_map/reshape;squeeze | solution.py:110
  370.9 0.4 fusion.8
  371.3 3.3 fusion.16
  374.6 0.3 fusion.19
  375.0 0.1 convert_element_type.54
  375.1 0.7 copy-done.1
  375.9 1.2 convolution_convert_fusion
  377.8 34.3 %all-reduce.2.cloned.1.call-done = bf16[2,32,1536]{2,1,0:T(8,128)(2,1)} async-done(((bf16[2,32,1536]{2,1,0:T(8,128)(2,1)}), bf16[2,32,1536]{2,1,0:T(8,128)(2,1)}) %all-reduce.2.cloned.1.call-update) | async-done | bytes 196624 | tf_op jit(solution)/shard_map/psum | solution.py:141
  412.1 1.1 fusion.38
  413.2 1.1 multiply_reduce_fusion
  414.3 1.2 broadcast_multiply_fusion
  415.5 0.1 mul.213
  415.6 0.1 mul.214
  415.7 0.6 fusion.55
  (31 shorter events, 0.2 us)
Async XLA Ops:
  7.2 4.9 %copy-start = (f32[16,5,1536]{2,0,1:T(8,128)S(1)}, f32[16,5,1536]{2,0,1:T(8,128)}, u32[]{:S(2)}) copy-start(f32[16,5,1536]{2,0,1:T(8,128)} %param.16) | copy-start | bytes 1474564
  7.2 4.9 %copy-start.4 = (s32[2]{0:T(128)S(1)}, s32[2]{0:T(128)}, u32[]{:S(2)}) copy-start(s32[2]{0:T(128)} %param.14) | copy-start | bytes 28
  7.2 142.2 %all-gather.5.cloned.1.call-start = ((), (), s32[]{:S(2)}) async-start(), calls=%async_computation | async-start | bytes 4737024 | tf_op jit(solution)/shard_map/all_gather | solution.py:81
  8.6 256.3 %all-gather.9.cloned.1.call-start = ((), (), s32[]{:S(2)}) async-start(), calls=%async_computation.3 | async-start | bytes 1579008 | tf_op jit(solution)/shard_map/all_gather | solution.py:138
  9.4 345.0 %all-gather.7.cloned.1.call-start = ((), (), s32[]{:S(2)}) async-start(), calls=%async_computation.1 | async-start | bytes 3244032 | tf_op jit(solution)/shard_map/all_gather | solution.py:104
  149.4 3.9 copy-start.5
  149.4 3.9 copy-start.6
  149.4 4.1 copy-start.2
  153.2 258.9 %all-reduce.2.cloned.1.call-start = ((), (), s32[]{:S(2)}) async-start(), calls=%async_computation.2 | async-start | bytes 393216 | tf_op jit(solution)/shard_map/psum | solution.py:141
  374.6 1.3 copy-start.1
  375.0 39.3 %copy-start.7 = (bf16[1536,64]{0,1:T(8,128)(2,1)S(1)}, bf16[1536,64]{0,1:T(8,128)(2,1)}, u32[]{:S(2)}) copy-start(bf16[1536,64]{0,1:T(8,128)(2,1)} %param.21) | copy-start | bytes 589828
  377.0 38.7 %copy-start.3 = (f32[2,1,2048]{2,1,0:T(1,128)S(1)}, f32[2,1,2048]{2,1,0:T(1,128)}, u32[]{:S(2)}) copy-start(f32[2,1,2048]{2,1,0:T(1,128)} %param.11) | copy-start | bytes 49156
Sparse Core Ops, SparseCore 0:
  12.5 136.7 all-gather.4
  153.5 111.3 all-gather.8
  268.3 86.0 all-gather.6
  377.2 34.8 all-reduce.1
where the time goes:
time: 423 us
  waiting for transfers between devices  367 us (87%)
  local copies, waits for them, and re-layouts  21.5 us (5%)
  between operations  14.8 us (3%)
  matrix products  14.3 us (3%)
  other arithmetic  5.08 us (1%)
    all_gather x1, waiting for transfers between devices, body(): lax.all_gather(qkv_weight, ('item', 'rows'), axis=1, tiled=True)  137 us
    all_gather x1, waiting for transfers between devices, body(): lax.all_gather(out_weight, ('item', 'rows'), axis=1, tiled=True)  110 us
    all_gather x1, waiting for transfers between devices, body(): gathered = lax.all_gather(image_kv, 'rows', axis=2, tiled=True)  85.4 us
    psum x1, waiting for transfers between devices, body(): lax.psum(partial_value.astype(jnp.bfloat16), 'hid').astype(jnp.float32)  34.3 us
  transfers between devices with their start and end apart: 4, of which 4 were waited for; matrix products, arithmetic and copies ran while one was open for 3% of the time, Pallas kernels for 0%

commit v1 on v0

--- a/solution.py
+++ b/solution.py
@@ -1,3 +1,4 @@
+import functools
 import jax
 import jax.numpy as jnp
 from jax import lax
@@ -5,6 +6,13 @@
 
 HD = 64
 STEPS = 28
+
+
+def form_the_tables(arr_in, along_axis):
+    return lax.all_gather(arr_in, axis_name=along_axis).sum(axis=0)
+
+
+launch_rails_now = functools.partial(form_the_tables, along_axis="hid")
 
 
 def sigma_level(position):
@@ -138,7 +146,7 @@
         lax.all_gather(out_weight, ("item", "rows"), axis=1, tiled=True),
         preferred_element_type=jnp.float32,
     )
-    summed = lax.psum(partial_value.astype(jnp.bfloat16), "hid").astype(jnp.float32)
+    summed = launch_rails_now(partial_value.astype(jnp.bfloat16)).astype(jnp.float32)
     summed = summed.reshape(slot_count, per_slot, model_width)
     residual = embedded + conditions[:, 2:3, :] * summed
     final_in = (normalize(residual) * (1.0 + conditions[:, 4:5, :]) + conditions[:, 3:4, :]).astype(

time: 423 us -> 392 us (0.927)
  waiting for transfers between devices: 367 us -> 332 us
  blocking collectives: 0 us -> 6.92 us
    psum x1 -> x0, waiting for transfers between devices: 34.3 us -> none  [body(): lax.psum(partial_value.astype(jnp.bfloat16), 'hid').astype(jnp.float32)]
    all_gather x0 -> x1, blocking collectives: none -> 6.92 us  [form_the_tables(): return lax.all_gather(arr_in, axis_name=along_axis).sum(axis=0)]
  transfers between devices with their start and end apart: 4 -> 3, of which waited for: 4 -> 3; matrix products, arithmetic and copies ran while one was open for 3% -> 3% of each run, Pallas kernels for 0% -> 0%
where the time goes in v1:
time: 392 us; the launch traced here: 391 us
  waiting for transfers between devices  332 us (85%)
  local copies, waits for them, and re-layouts  21.5 us (5%)
  between operations  14.8 us (4%)
  matrix products  12.7 us (3%)
  blocking collectives  6.92 us (2%)
    all_gather x1, waiting for transfers between devices, body(): lax.all_gather(qkv_weight, ('item', 'rows'), axis=1, tiled=True)  137 us
    all_gather x1, waiting for transfers between devices, body(): lax.all_gather(out_weight, ('item', 'rows'), axis=1, tiled=True)  109 us
    all_gather x1, waiting for transfers between devices, body(): gathered = lax.all_gather(image_kv, 'rows', axis=2, tiled=True)  85.4 us
  transfers between devices with their start and end apart: 3, of which 3 were waited for; matrix products, arithmetic and copies ran while one was open for 3% of the time, Pallas kernels for 0%

profile of v1, /device:TPU:1, one launch (start us, length us, event | category | flops | bytes accessed | tf_op | source)
XLA Modules:
  0.0 391.4 jit_solution(8724827226614394941)
XLA Ops:
  7.2 0.0 all-gather.6.cloned.1.call-start
  7.2 1.4 copy.35
  8.6 0.0 all-gather.6.cloned.1.call-update
  8.6 0.0 all-gather.10.cloned.1.call-start
  8.7 0.7 all-gather.10.cloned.1.call-update
  9.4 0.0 all-gather.8.cloned.1.call-start
  9.5 0.1 fusion.51
  9.5 0.2 fusion.44
  9.8 0.8 convert_reduce_fusion
  10.6 0.1 convert_element_type.54
  10.7 1.2 fusion.58
  11.9 0.2 multiply_reduce_fusion.1
  12.1 0.3 fusion.25
  12.4 0.1 add_convert_fusion.1
  12.6 136.8 %all-gather.6.cloned.1.call-done = bf16[3,1536,384]{2,0,1:T(4,128)(2,1)} async-done(((bf16[3,6,384]{2,0,1:T(4,128)(2,1)}), bf16[3,1536,384]{2,0,1:T(4,128)(2,1)}) %all-gather.6.cloned.1.call-update) | async-done | bytes 3538960 | tf_op jit(solution)/shard_map/all_gather | solution.py:89
  149.4 3.1 fusion.20
  152.5 0.6 slice.48
  153.1 0.0 all-gather.8.cloned.1.call-update
  153.9 0.1 broadcast_and_fusion.1
  153.9 0.1 broadcast_and_fusion
  154.0 0.1 and.40
  154.1 0.7 fusion.56
  154.8 0.5 copy.37
  155.3 0.5 copy.39
  155.9 109.1 %all-gather.10.cloned.1.call-done = bf16[256,6,384]{2,1,0:T(8,128)(2,1)} async-done(((bf16[1,6,384]{2,1,0:T(8,128)(2,1)}), bf16[256,6,384]{2,1,0:T(8,128)(2,1)}) %all-gather.10.cloned.1.call-update) | async-done | bytes 1179664 | tf_op jit(solution)/shard_map/all_gather | solution.py:146
  265.0 3.3 reshape.277
  268.3 0.1 reshape_squeeze.15
  268.4 0.3 fusion.59
  268.7 0.2 fusion.29
  268.9 85.4 %all-gather.8.cloned.1.call-done = bf16[2,2,32,32,384]{4,3,2,1,0:T(8,128)(2,1)} async-done(((bf16[2,2,1,32,384]{4,3,2,1,0:T(8,128)(2,1)}), bf16[2,2,32,32,384]{4,3,2,1,0:T(8,128)(2,1)}) %all-gather.8.cloned.1.call-update) | async-done | bytes 3145744 | tf_op jit(solution)/shard_map/all_gather | solution.py:112
  354.4 3.5 fusion.55
  357.8 3.7 reshape_squeeze.18
  361.6 3.4 fusion.60
  365.0 5.9 %reshape_squeeze.19 = bf16[2,1024,6,64]{3,2,1,0:T(8,128)(2,1)} reshape(bf16[1,2,32,32,384]{4,3,2,1,0:T(8,128)(2,1)} %get-tuple-element.5) | data formatting | bytes 3145728 | tf_op jit(solution)/shard_map/reshape;squeeze | solution.py:118
  370.9 0.4 fusion.8
  371.3 3.3 fusion.16
  374.6 0.3 fusion.19
  375.0 0.1 convert_element_type.62
  375.1 0.7 copy-done.1
  375.9 0.5 convolution_convert_fusion
  376.4 6.9 %all-gather = bf16[128,1536]{1,0:T(8,128)(2,1)S(1)} all-gather(bf16[64,1536]{1,0:T(8,128)(2,1)S(1)} %convolution_convert_fusion), channel_id=2, replica_groups=mesh['item'=8,'rows'=32,'hid'=2] {'hid'}, dimensions={0}, use_global_device_ids=true | all-gather | bytes 589824 | tf_op jit(solution)/shard_map/all_gather | solution.py:12
  383.3 0.1 reduce_sum.76
  383.4 0.1 fusion.40
  383.5 0.2 multiply_reduce_fusion
  383.7 0.3 broadcast_multiply_fusion
  384.0 0.1 mul.213
  384.1 0.1 mul.214
  384.2 0.6 fusion.57
  (30 shorter events, 0.2 us)
Async XLA Ops:
  7.2 4.9 %copy-start = (f32[16,5,1536]{2,0,1:T(8,128)S(1)}, f32[16,5,1536]{2,0,1:T(8,128)}, u32[]{:S(2)}) copy-start(f32[16,5,1536]{2,0,1:T(8,128)} %param.16) | copy-start | bytes 1474564
  7.2 4.9 %copy-start.4 = (s32[2]{0:T(128)S(1)}, s32[2]{0:T(128)}, u32[]{:S(2)}) copy-start(s32[2]{0:T(128)} %param.14) | copy-start | bytes 28
  7.2 142.2 %all-gather.6.cloned.1.call-start = ((), (), s32[]{:S(2)}) async-start(), calls=%async_computation | async-start | bytes 4737024 | tf_op jit(solution)/shard_map/all_gather | solution.py:89
  8.6 256.3 %all-gather.10.cloned.1.call-start = ((), (), s32[]{:S(2)}) async-start(), calls=%async_computation.2 | async-start | bytes 1579008 | tf_op jit(solution)/shard_map/all_gather | solution.py:146
  9.4 345.0 %all-gather.8.cloned.1.call-start = ((), (), s32[]{:S(2)}) async-start(), calls=%async_computation.1 | async-start | bytes 3244032 | tf_op jit(solution)/shard_map/all_gather | solution.py:112
  149.4 4.5 %copy-start.5 = (s32[2]{0:T(128)S(1)}, s32[2]{0:T(128)}, u32[]{:S(2)}) copy-start(s32[2]{0:T(128)} %param.12) | copy-start | bytes 28
  149.4 4.5 %copy-start.6 = (s32[2]{0:T(128)S(1)}, s32[2]{0:T(128)}, u32[]{:S(2)}) copy-start(s32[2]{0:T(128)} %param.13) | copy-start | bytes 28
  149.4 4.7 %copy-start.2 = (bf16[2,2,154,384]{3,1,2,0:T(2,128)(2,1)S(1)}, bf16[2,2,154,384]{3,1,2,0:T(2,128)(2,1)}, u32[]{:S(2)}) copy-start(bf16[2,2,154,384]{3,1,2,0:T(2,128)(2,1)} %param.17) | copy-start | bytes 1419268
  374.6 1.3 copy-start.1
  375.9 7.9 %copy-start.7 = (bf16[1536,64]{0,1:T(8,128)(2,1)S(1)}, bf16[1536,64]{0,1:T(8,128)(2,1)}, u32[]{:S(2)}) copy-start(bf16[1536,64]{0,1:T(8,128)(2,1)} %param.21) | copy-start | bytes 589828
  383.3 0.9 copy-start.3
Sparse Core Ops, SparseCore 0:
  12.5 136.7 all-gather.5
  153.5 111.3 all-gather.9
  268.3 86.0 all-gather.7
